TPU v7x, 256 devices: a whole 4x4x8 slice. The times are simulated.
256 devices in a mesh: copy: 2 (over y_hi), dp: 8 (over x, core), fsdp: 16 (over y_lo, z).
Axes of the slice: x: 4, y: 4 (y_hi: 2, y_lo: 2; y = y_hi * 2 + y_lo), z: 8, core: 2. Of those that a mesh axis runs over, the one named last changes fastest.
Arguments:
- queries: bfloat16 [2, 128, 256, 2560], P('copy', ('dp', 'fsdp')), may hold values from -25 to 25
- keys: bfloat16 [2, 128, 256, 2560], P('copy', ('dp', 'fsdp')), may hold values from -25 to 25
- values: bfloat16 [2, 128, 256, 2560], P('copy', ('dp', 'fsdp')), may hold values from -6 to 6
- residual: bfloat16 [2, 128, 256, 2560], P('copy', ('dp', 'fsdp')), may hold values from -6 to 6
- event_ids: int32 [128, 256], P(('dp', 'fsdp')), may hold values from 0 to 1023
- lengths: int32 [128], replicated, may hold values from 8 to 256, as said below
- type_weight: float32 [1024], replicated, may hold values from 0.25 to 4
- w_out: bfloat16 [2, 2560, 2560], P('copy', 'fsdp'), may hold values from -0.125 to 0.125
- gain: float32 [2, 2560], P('copy'), may hold values from 0.5 to 1.5
Outputs:
- loss: float32 [2, 128], P('copy', ('dp', 'fsdp'))
- d_queries: bfloat16 [2, 128, 256, 2560], P('copy', ('dp', 'fsdp'))
- d_keys: bfloat16 [2, 128, 256, 2560], P('copy', ('dp', 'fsdp'))
- d_values: bfloat16 [2, 128, 256, 2560], P('copy', ('dp', 'fsdp'))
- d_wo: float32 [2, 2560, 2560], P('copy', 'fsdp')
Inputs may be any that keep to these rules, and one draw needn't show every extreme that they name: `lengths`: every history has at least 8 valid events and some history has all 256.
All inputs are finite; a program needn't handle non-finite values.
Results may differ from a plain program's by a relative error of at most 0.02.
Values may be sent and summed in bfloat16 or wider, within the bound.
A program may use at most 128 MiB of HBM per device.

v0:
```python
import jax
import jax.numpy as jnp
from jax import lax
from jax.experimental import pallas as pl
from jax.experimental.pallas import tpu as pltpu
from jax.sharding import PartitionSpec as P

MESH = pl.DeviceIdType.MESH
F32 = jnp.float32
BF16 = jnp.bfloat16
L, D, H, DH = 256, 2560, 20, 128
BLK = 160
HALF = 80
QW = 640
CW = 1280
AW, BW = 256, 384
SCALE = 128.0**0.5
NT = (((1,), (1,)), ((), ()))
TN = (((0,), (0,)), ((), ()))
NEAR = (0, -1, 1, -2, 2, -3, 3, -4)


def dot(a, b, dims=(((1,), (0,)), ((), ()))):
    return lax.dot_general(a, b, dims, preferred_element_type=F32)


def kernel(
    q_hbm, k_hbm, v_hbm, res_hbm, w_ref, ids_ref, len_ref, tw_ref, gain_ref,
    loss_ref, dq_ref, dk_ref, dv_ref, dwo_ref,
    q_ref, k_ref, v_ref, res_ref, wf, at, hid, pb, gp, dh, dhs, probs, bias, pbuf, za, zaf, xa, xb, zb, fsum, yrx, rows, dab, ivs, ivr, acc,
    s_send, s_zr, s_xr, s_yr, s_sib, s_pr, s_misc, s_za, s_xa, s_xb, s_zb, s_fin, s_in,
):
    attn, hb = dk_ref, dq_ref
    c = lax.axis_index("copy")
    d = lax.axis_index("dp")
    f = lax.axis_index("fsdp")
    x, core = d // 2, d % 2
    y, z = f // 8, f % 8
    own = d * 16 + f

    def at_z(step):
        return (c, d, y * 8 + (z + step + 8) % 8)

    def at_x(step):
        return (c, ((x + step + 4) % 4) * 2 + core, f)

    other_y = (c, d, (1 - y) * 8 + z)
    sibling = (c, x * 2 + 1 - core, f)
    partner = (1 - c, d, f)

    def send(src, dst, group, recv, device):
        copy = pltpu.make_async_remote_copy(
            src_ref=src, dst_ref=dst, send_sem=s_send.at[group], recv_sem=recv,
            device_id=device, device_id_type=MESH,
        )
        copy.start()

    def arrived(ref, sem):
        pltpu.make_async_copy(ref, ref, sem).wait()

    loads = [
        pltpu.make_async_copy(src, dst, s_in.at[i])
        for i, (src, dst) in enumerate(
            ((q_hbm, q_ref), (k_hbm, k_ref), (v_hbm, v_ref), (res_hbm, res_ref))
        )
    ]
    for load in loads:
        load.start()

    barrier = pltpu.get_barrier_semaphore()
    greet = (at_z(1), at_z(-1), at_x(1), at_x(-1), at_x(2), other_y, sibling, partner)
    for device in greet:
        pl.semaphore_signal(barrier, inc=1, device_id=device, device_id_type=MESH)
    pl.semaphore_wait(barrier, len(greet))

    STREAMS = ((0, 0, 256), (0, 256, 384), (1, 0, QW), (-1, 0, QW), (2, 0, 384), (2, 384, 256))

    def part_cols(quarter, lo, width):
        return pl.ds(pl.multiple_of(((quarter + 8) % 4) * QW + lo, 128), width)

    def piece(yy, zz, quarter, lo=0, width=QW):
        row = pl.multiple_of((yy * 8 + (zz + 16) % 8) * BLK + core * HALF, 16)
        return wf.at[pl.ds(row, HALF), part_cols(quarter, lo, width)]

    def own_piece(s):
        step, lo, width = STREAMS[s]
        row = pl.ds(pl.multiple_of(core * HALF, 16), HALF)
        return w_ref.at[row, part_cols(x + step, lo, width)]

    def stream_piece(s, yy, zz):
        step, lo, width = STREAMS[s]
        return piece(yy, zz, x + step, lo, width)

    def steps(s, way):
        return 4 if (s + way) % 2 == 0 else 3

    def to_sibling(ref, s):
        send(ref, ref, 0, s_sib.at[s], sibling)

    def z_event(s, k):
        for way, sign in ((0, 1), (1, -1)):
            last = steps(s, way)
            if 0 < k <= last:
                got = stream_piece(s, y, z - sign * k)
                arrived(got, s_zr.at[s, way, k - 1])
                if k < last:
                    send(got, got, 0, s_zr.at[s, way, k], at_z(sign))
                if s < 2:
                    m = NEAR.index(-sign * k) if k < 4 else 7
                    send(got, got, 0, s_yr.at[s, m], other_y)
                to_sibling(got, s)
            elif k == 0:
                dst = stream_piece(s, y, z)
                send(own_piece(s), dst, 0, s_zr.at[s, way, 0], at_z(sign))

    def y_event(s, m):
        got = stream_piece(s, 1 - y, z + NEAR[m])
        arrived(got, s_yr.at[s, m])
        if s == 1:
            both = piece(1 - y, z + NEAR[m], x)
            send(both, both, 0, s_xr.at[0, m], at_x(1))
            send(both, both, 0, s_xr.at[1, m], at_x(-1))
        to_sibling(got, s)

    def x_event(m):
        for way, sign in ((0, 1), (1, -1)):
            got = piece(1 - y, z + NEAR[m], x - sign)
            arrived(got, s_xr.at[way, m])
            if m % 2 == way:
                for i in (0, 1):
                    got_i = piece(1 - y, z + NEAR[m], x - sign, *STREAMS[4 + i][1:])
                    send(got_i, got_i, 0, s_xr.at[way, 8 + 4 * i + m // 2], at_x(sign))
            to_sibling(got, 2 if way == 1 else 3)

    def x_last(n, i):
        for way in (0, 1):
            got = piece(1 - y, z + NEAR[2 * n + way], x + 2, *STREAMS[4 + i][1:])
            arrived(got, s_xr.at[way, 8 + 4 * i + n])
            to_sibling(got, 4 + i)

    for s in (0, 1):
        z_event(s, 0)
        send(own_piece(s), stream_piece(s, y, z), 0, s_yr.at[s, 0], other_y)
    z_event(2, 0)
    send(gain_ref, gp, 1, s_misc.at[0], partner)
    local = pltpu.make_async_copy(
        w_ref, wf.at[pl.ds(pl.multiple_of(f * BLK, 16), BLK), :], s_misc.at[2]
    )
    local.start()

    lane = lax.broadcasted_iota(jnp.int32, (1, 128), 1)
    lens = len_ref[...]
    count = jnp.sum(lens).astype(F32)
    length = jnp.sum(jnp.where(lane == own, lens, 0), axis=-1, keepdims=True)
    r_at = lax.broadcasted_iota(jnp.int32, (L, L), 0)
    c_at = lax.broadcasted_iota(jnp.int32, (L, L), 1)
    bias[...] = jnp.where((c_at <= r_at) & (c_at < length), F32(0.0), F32(-1e30))

    def head(h):
        return pl.ds(pl.multiple_of(h * DH, DH), DH)

    def forward(h, carry):
        cols = head(h)
        s = dot(q_ref[:, cols], k_ref[:, cols], NT) * F32(1.0 / SCALE) + bias[...]
        e = jnp.exp(s - jnp.max(s, axis=-1, keepdims=True))
        p = (e / jnp.sum(e, axis=-1, keepdims=True)).astype(BF16)
        probs[h] = p
        a = dot(p, v_ref[:, cols])
        attn[:, cols] = a.astype(BF16)
        at[cols, 0:L] = a.T.astype(BF16)
        return carry

    def heads(first, n):
        lax.fori_loop(first, first + n, forward, 0)

    for load in loads[:3]:
        load.wait()
    heads(0, 2)
    for k in (1, 2, 3):
        z_event(0, k)
        y_event(0, 2 * k - 2)
        z_event(1, k)
        y_event(1, 2 * k - 2)
        if k == 3:
            z_event(3, 0)
        z_event(2, k)
        heads(6 * k - 4, 3)
        y_event(0, 2 * k - 1)
        y_event(1, 2 * k - 1)
        if k > 1:
            x_event(2 * k - 4)
            x_event(2 * k - 3)
        heads(6 * k - 1, 3)
    z_event(0, 4)
    y_event(0, 6)
    z_event(1, 4)
    y_event(1, 6)
    z_event(3, 1)
    z_event(4, 0)
    z_event(2, 4)
    z_event(5, 0)
    x_event(4)
    y_event(0, 7)
    y_event(1, 7)
    send(at.at[:, 0:L], at.at[:, L : 2 * L], 1, s_misc.at[1], sibling)

    type_at = lax.broadcasted_iota(jnp.int32, (1, 1024), 1).astype(F32)
    ids = jnp.broadcast_to(ids_ref[...].astype(F32), (128, L)).T[:, 0:1]
    looked = jnp.sum(
        jnp.where(ids == type_at, tw_ref[...], F32(0.0)), axis=-1, keepdims=True
    )
    live = lax.broadcasted_iota(jnp.int32, (L, 1), 0) < length
    rows[:, 0:1] = jnp.where(live, looked, F32(0.0))
    rows[:, 1:2] = jnp.zeros((L, 1), F32)
    local.wait()
    loads[3].wait()

    def stream_cols(s):
        step, lo, width = STREAMS[s]
        return part_cols(x + step, lo, width)

    def hidden(s):
        arrived(wf.at[0 : 15 * HALF, 0 : STREAMS[s][2]], s_sib.at[s])
        cols = stream_cols(s)
        hc = res_ref[:, cols].astype(F32) + dot(attn[...], wf[:, cols])
        hid[:, cols] = hc
        hb[:, cols] = hc.astype(BF16)
        rows[:, 1:2] += jnp.sum(hc * hc, axis=-1, keepdims=True)
        if s == 5:
            inv = lax.rsqrt(rows[:, 1:2] * F32(1.0 / D) + F32(1e-06))
            ivs[...] = jnp.broadcast_to(inv, (L, 128)).T[0:8]
            send(ivs, ivr, 1, s_misc.at[4], partner)
        send(hb.at[:, cols], pb.at[:, cols], 2, s_pr.at[s], partner)

    hidden(0)
    z_event(3, 2)
    x_event(5)
    z_event(4, 1)
    z_event(5, 1)
    hidden(1)
    x_event(6)
    z_event(3, 3)
    x_event(7)
    z_event(4, 2)
    z_event(5, 2)
    hidden(2)
    z_event(3, 4)
    z_event(4, 3)
    hidden(3)
    z_event(5, 3)
    for n in range(4):
        x_last(n, 0)
    z_event(4, 4)
    hidden(4)
    for n in range(4):
        x_last(n, 1)
    z_event(5, 4)
    hidden(5)
    arrived(gp, s_misc.at[0])
    arrived(at.at[:, L : 2 * L], s_misc.at[1])
    arrived(ivr, s_misc.at[4])

    tok = rows[:, 0:1]
    inv = lax.rsqrt(rows[:, 1:2] * F32(1.0 / D) + F32(1e-06))
    inv_p = jnp.broadcast_to(ivr[0:1, :], (128, L)).T[:, 0:1]
    coef = 2.0 * tok / (D * count)
    acc[...] = jnp.zeros((2, L, 128), F32)

    for s in range(6):
        arrived(pb.at[:, stream_cols(s)], s_pr.at[s])
        step, lo, width = STREAMS[s]

        def stats(t, carry):
            at_col = ((x + step + 8) % 4) * QW + lo + t * 128
            cols = pl.ds(pl.multiple_of(at_col, 128), 128)
            n = hid[:, cols] * inv
            g = gain_ref[:, cols]
            diff = n * g - pb[:, cols].astype(F32) * inv_p * gp[:, cols]
            acc[0] += diff * diff
            acc[1] += n * (diff * g)
            return carry

        lax.fori_loop(0, width // 128, stats, 0)
    rows[:, 3:4] = jnp.sum(acc[0], axis=-1, keepdims=True)
    rows[:, 4:5] = jnp.sum(acc[1], axis=-1, keepdims=True)
    loss_ref[...] = jnp.sum(tok * rows[:, 3:4], axis=0, keepdims=True) / (D * count)
    mean = rows[:, 4:5] * F32(1.0 / D)

    def grads(t, carry):
        cols = pl.ds(pl.multiple_of(((1 - core) * CW + t * 256) % D, 256), 256)
        n = hid[:, cols] * inv
        g = gain_ref[:, cols]
        diff = n * g - pb[:, cols].astype(F32) * inv_p * gp[:, cols]
        dh[:, cols] = (inv * coef * (diff * g - n * mean)).astype(BF16)
        return carry

    lax.fori_loop(0, 5, grads, 0)
    other_half = pl.ds(pl.multiple_of((1 - core) * CW, 128), CW)
    send(dh.at[:, other_half], dhs, 1, s_misc.at[3], sibling)
    lax.fori_loop(5, 10, grads, 0)
    arrived(dhs, s_misc.at[3])

    def term(row, n_rows, col, width):
        r = pl.ds(pl.multiple_of(row, 16), n_rows)
        mine = dh[:, pl.ds(pl.multiple_of(core * CW + col, 128), width)]
        theirs = dhs[:, pl.ds(pl.multiple_of(col, 128), width)]
        return dot(at[r, 0:L], mine) + dot(at[r, L : 2 * L], theirs)

    def block_row(yy, zz):
        return (yy * 8 + (zz + 16) % 8) * BLK

    WAYS = ((0, 1), (1, -1))

    def b_first(t):
        for way, sign in WAYS:
            for yy in (0, 1):
                val = term(block_row(yy, z - sign * (1 + t)), BLK, 2 * AW + way * BW, BW)
                pbuf[way, t, :, yy] = val.reshape(4, 40, BW).astype(BF16)
            send(
                pbuf.at[way, t, (x - sign + 4) % 4], xb.at[way, 0, t], 4,
                s_xb.at[way, 0, t], at_x(sign),
            )

    def b_next(t, k):
        for way, sign in WAYS:
            slot = xb.at[way, k - 1, t]
            arrived(slot, s_xb.at[way, k - 1, t])
            mine = pbuf[way, t, (x - sign * (1 + k) + 8) % 4]
            slot[...] = (slot[...].astype(F32) + mine.astype(F32)).astype(BF16)
            send(slot, xb.at[way, k, t], 4, s_xb.at[way, k, t], at_x(sign))

    def b_sum(way, t):
        slot = xb.at[way, 2, t]
        arrived(slot, s_xb.at[way, 2, t])
        return slot[...].astype(F32) + pbuf[way, t, x].astype(F32)

    def b_z(t):
        for way, sign in WAYS:
            val = b_sum(way, t)
            slot = zb.at[way, t]

            @pl.when(t == 0)
            def _():
                slot[...] = val.astype(BF16)

            @pl.when(t > 0)
            def _():
                arrived(slot, s_zb.at[way, t])
                slot[...] = (slot[...].astype(F32) + val).astype(BF16)

            send(slot, zb.at[way, t + 1], 5, s_zb.at[way, t + 1], at_z(sign))

    def a_step(t, yy):
        hop, part = t // 2, t % 2
        for way, sign in WAYS:
            n = steps(yy, way)

            @pl.when(t < 2 * n)
            def _():
                val = term(block_row(yy, z + sign * (n - hop)), BLK, part * AW, AW)
                slot = za.at[way, yy, part, hop]

                @pl.when(hop == 0)
                def _():
                    slot[...] = val.astype(BF16)

                @pl.when(hop > 0)
                def _():
                    arrived(slot, s_za.at[way, yy, part, hop])
                    slot[...] = (slot[...].astype(F32) + val).astype(BF16)

                send(
                    slot, za.at[way, yy, part, hop + 1], 3,
                    s_za.at[way, yy, part, hop + 1], at_z(sign),
                )

    def a_last(part):
        for yy in (0, 1):
            val = term(block_row(yy, z), BLK, part * AW, AW)
            for way in (0, 1):
                n = steps(yy, way)
                slot = za.at[way, yy, part, n]
                arrived(slot, s_za.at[way, yy, part, n])
                val = val + slot[...].astype(F32)
            zaf[part, :, yy] = val.reshape(4, 40, AW).astype(BF16)
        sign = 1 - 2 * part
        send(zaf.at[part, (x - sign + 4) % 4], xa.at[part, 0], 6, s_xa.at[part, 0], at_x(sign))

    def a_next(way, k):
        sign = 1 - 2 * way
        slot = xa.at[way, k - 1]
        arrived(slot, s_xa.at[way, k - 1])
        mine = zaf[way, (x - sign * (1 + k) + 8) % 4]
        slot[...] = (slot[...].astype(F32) + mine.astype(F32)).astype(BF16)
        send(slot, xa.at[way, k], 6, s_xa.at[way, k], at_x(sign))

    def pair_in(t):
        cols2 = pl.ds(pl.multiple_of(t * 256, 256), 256)
        dab[...] = dot(dh[...], wf[cols2, :], NT).astype(BF16)

    def pair(t, j):
        if True:
            cols = pl.ds(pl.multiple_of(t * 256 + j * DH, DH), DH)
            da = dab[:, j * DH : (j + 1) * DH]
            p = probs[2 * t + j]
            dv_ref[:, cols] = dot(p, da, TN).astype(BF16)
            dprob = dot(da, v_ref[:, cols], NT)
            pf = p.astype(F32)
            delta = jnp.sum(dprob * pf, axis=-1, keepdims=True)
            ds = (pf * (dprob - delta) * F32(1.0 / SCALE)).astype(BF16)
            dq_ref[:, cols] = dot(ds, k_ref[:, cols]).astype(BF16)
            dk_ref[:, cols] = dot(ds, q_ref[:, cols], TN).astype(BF16)

    arrived(pb, s_send.at[2])

    def tick(t, carry):
        @pl.when(t < 8)
        def _():
            a_step(t, 0)
            b_first(t)

        @pl.when(t == 8)
        def _():
            a_last(1)
            a_next(0, 1)

        @pl.when(t == 9)
        def _():
            a_next(0, 2)
            a_next(1, 1)

        pair_in(t)

        @pl.when(t < 8)
        def _():
            a_step(t, 1)

        @pl.when(t == 7)
        def _():
            a_last(0)

        @pl.when((t >= 1) & (t < 9))
        def _():
            b_next(t - 1, 1)

        pair(t, 0)

        @pl.when((t >= 2) & (t < 10))
        def _():
            b_next(t - 2, 2)

        @pl.when((t >= 3) & (t < 10))
        def _():
            b_z(t - 3)

        pair(t, 1)
        return carry

    lax.fori_loop(0, 10, tick, 0)
    a_next(1, 2)

    PARTS = ((0, 2 * AW), (2 * AW, 2 * BW))

    def to_y(part):
        lo, width = PARTS[part]
        send(
            fsum.at[1 - y, :, lo : lo + width], yrx.at[:, lo : lo + width], 7,
            s_fin.at[part, 0], other_y,
        )

    def place(part, quarter, of_core):
        lo, width = PARTS[part]
        cols = pl.ds(pl.multiple_of(of_core * CW + lo, 128), width)
        return dwo_ref.at[(quarter + 4) % 4, :, cols]

    def from_y(part):
        lo, width = PARTS[part]
        got = yrx.at[:, lo : lo + width]
        arrived(got, s_fin.at[part, 0])
        mine = place(part, x, core)
        mine[...] = (got[...].astype(F32) + fsum[y, :, lo : lo + width].astype(F32)).astype(BF16)
        for i, step in enumerate((1, -1, 2)):
            send(mine, mine, 7, s_fin.at[part, 1 + i], at_x(step))
        send(mine, mine, 7, s_fin.at[part, 4], sibling)

    def from_x(part):
        for i, step in enumerate((1, -1, 2)):
            got = place(part, x - step, core)
            arrived(got, s_fin.at[part, 1 + i])
            send(got, got, 7, s_fin.at[part, 5 + i], sibling)

    def from_sibling(part):
        for i, step in enumerate((0, 1, -1, 2)):
            arrived(place(part, x - step, 1 - core), s_fin.at[part, 4 + i])

    for way, sign in WAYS:
        slot = xa.at[way, 2]
        arrived(slot, s_xa.at[way, 2])
        val = slot[...].astype(F32) + zaf[way, x].astype(F32)
        fsum[:, :, way * AW : (way + 1) * AW] = val.astype(BF16)
    to_y(0)
    for way, sign in WAYS:
        val = b_sum(way, 7)
        slot = zb.at[way, 7]
        arrived(slot, s_zb.at[way, 7])
        lo = 2 * AW + way * BW
        fsum[:, :, lo : lo + BW] = (slot[...].astype(F32) + val).astype(BF16)
    to_y(1)
    from_y(0)
    from_y(1)
    from_x(0)
    from_x(1)
    from_sibling(0)
    from_sibling(1)

    arrived(wf.at[0 : 32 * HALF, 0:QW], s_send.at[0])
    arrived(wf.at[0 : 32 * HALF, 0:QW], s_send.at[0])
    arrived(wf.at[0 : 32 * HALF, 0:QW], s_send.at[0])
    arrived(wf.at[0 : 24 * HALF, 0:QW], s_send.at[0])
    arrived(gp, s_send.at[1])
    arrived(ivr, s_send.at[1])
    arrived(at.at[:, 0:L], s_send.at[1])
    arrived(dhs, s_send.at[1])
    for way in (0, 1):
        for yy in (0, 1):
            arrived(za.at[way, yy, :, 1 : steps(yy, way) + 1], s_send.at[3])
        arrived(xb.at[way], s_send.at[4])
        arrived(zb.at[way, 1:8], s_send.at[5])
        arrived(xa.at[way], s_send.at[6])
    for _ in range(8):
        arrived(yrx, s_send.at[7])


def finish(
    loss_in, dq, dk, dv, dwo, loss_out, dq_out, dk_out, dv_out, dwo_out, dwo_f, s_out
):
    given = []
    for i, (src, dst) in enumerate(((dq, dq_out), (dk, dk_out), (dv, dv_out), (dwo_f, dwo_out))):
        if i == 3:
            dwo_f[...] = dwo[...].astype(F32).reshape(BLK, D)
        given.append(pltpu.make_async_copy(src, dst, s_out.at[i]))
        given[-1].start()
    loss_out[...] = loss_in[...]
    for copy in given:
        copy.wait()


def body(queries, keys, values, residual, event_ids, lengths, type_weight, w_out, gain):
    vmem = pl.BlockSpec(memory_space=pltpu.VMEM)
    hbm = pl.BlockSpec(memory_space=pl.ANY)
    dma = pltpu.SemaphoreType.DMA
    big = jax.ShapeDtypeStruct((L, D), BF16)
    near = pltpu.VMEM((L, D), BF16)
    loss, dq, dk, dv, dwo = pl.pallas_call(
        kernel,
        out_shape=(
            jax.ShapeDtypeStruct((1, 1), F32), near, near, near,
            pltpu.VMEM((4, 40, D), BF16),
        ),
        in_specs=[hbm] * 5 + [vmem] * 4,
        out_specs=(vmem,) * 5,
        scratch_shapes=[pltpu.VMEM((L, D), BF16)] * 4
        + [
            pltpu.VMEM((D, D), BF16),
            pltpu.VMEM((D, 2 * L), BF16),
            pltpu.VMEM((L, D), F32),
            pltpu.VMEM((L, D), BF16),
            pltpu.VMEM((1, D), F32),
            pltpu.VMEM((L, D), BF16),
            pltpu.VMEM((L, CW), BF16),
            pltpu.VMEM((H, L, L), BF16),
            pltpu.VMEM((L, L), F32),
            pltpu.VMEM((2, 8, 4, 2, 40, BW), BF16),
            pltpu.VMEM((2, 2, 2, 5, BLK, AW), BF16),
            pltpu.VMEM((2, 4, 2, 40, AW), BF16),
            pltpu.VMEM((2, 3, 2, 40, AW), BF16),
            pltpu.VMEM((2, 3, 8, 2, 40, BW), BF16),
            pltpu.VMEM((2, 8, 2, 40, BW), BF16),
            pltpu.VMEM((2, 40, CW), BF16),
            pltpu.VMEM((40, CW), BF16),
            pltpu.VMEM((L, 128), F32),
            pltpu.VMEM((L, 256), BF16),
            pltpu.VMEM((8, L), F32),
            pltpu.VMEM((8, L), F32),
            pltpu.VMEM((2, L, 128), F32),
            dma((8,)),
            dma((6, 2, 4)),
            dma((2, 16)),
            dma((2, 8)),
            dma((6,)),
            dma((6,)),
            dma((5,)),
            dma((2, 2, 2, 5)),
            dma((2, 3)),
            dma((2, 3, 8)),
            dma((2, 8)),
            dma((2, 8)),
            dma((4,)),
        ],
        compiler_params=pltpu.CompilerParams(
            collective_id=0, has_side_effects=True, vmem_limit_bytes=58 * 1024 * 1024
        ),
        name="step",
    )(
        queries[0, 0], keys[0, 0], values[0, 0], residual[0, 0], w_out[0],
        event_ids, lengths.reshape(1, 128), type_weight.reshape(1, 1024), gain,
    )
    loss, dq, dk, dv, dwo = pl.pallas_call(
        finish,
        out_shape=(
            jax.ShapeDtypeStruct((1, 1), F32), big, big, big, jax.ShapeDtypeStruct((BLK, D), F32)
        ),
        in_specs=[vmem] * 5,
        out_specs=(vmem, hbm, hbm, hbm, hbm),
        scratch_shapes=[pltpu.VMEM((BLK, D), F32), dma((4,))],
        compiler_params=pltpu.CompilerParams(vmem_limit_bytes=4 * 1024 * 1024),
        name="finish",
    )(loss, dq, dk, dv, dwo)
    return loss, dq[None, None], dk[None, None], dv[None, None], dwo[None]


def solution(mesh):
    hist = P("copy", ("dp", "fsdp"), None, None)
    return jax.shard_map(
        body,
        mesh=mesh,
        in_specs=(
            hist, hist, hist, hist, P(("dp", "fsdp"), None), P(), P(),
            P("copy", "fsdp", None), P("copy", None),
        ),
        out_specs=(
            P("copy", ("dp", "fsdp")), hist, hist, hist, P("copy", "fsdp", None),
        ),
        check_vma=False,
    )
```

profile of v0, /device:TPU:1, one launch (start us, length us, event | category | flops | bytes accessed | tf_op | source)
XLA Modules:
  0.0 136.9 jit_solution(3749319506261373351)
XLA Ops:
  0.6 132.6 %step.1 = (f32[1,1]{1,0:T(1,128)}, bf16[256,2560]{1,0:T(8,128)(2,1)S(1)}, bf16[256,2560]{1,0:T(8,128)(2,1)S(1)}, bf16[256,2560]{1,0:T(8,128)(2,1)S(1)}, bf16[4,40,2560]{2,1,0:T(8,128)(2,1)S(1)}) custom-call(bf16[256,2560]{1,0:T(8,128)(2,1)} %bitcast.11, bf16[256,2560]{1,0:T(8,128)(2,1)} %bitcast.12, bf16[256,2560]{1,0:T(8,128)(2,1)} %bitcast.13, ...), custom_call_target="tpu_custom_call" | custom-call | tf_op jit(solution)/shard_map/step/pallas_call | solution.py:554
  133.3 3.6 %finish.1 = (f32[1,1]{1,0:T(1,128)}, bf16[256,2560]{1,0:T(8,128)(2,1)}, bf16[256,2560]{1,0:T(8,128)(2,1)}, bf16[256,2560]{1,0:T(8,128)(2,1)}, f32[160,2560]{1,0:T(8,128)}) custom-call(f32[1,1]{1,0:T(1,128)} %get-tuple-element.15.loss_in, bf16[256,2560]{1,0:T(8,128)(2,1)S(1)} %get-tuple-element.16.dq, bf16[256,2560]{1,0:T(8,128)(2,1)S(1)} %get-tuple-element.17.dk, ...), custom_call_target="tpu_custom_call" | custom-call | tf_op jit(solution)/shard_map/finish/pallas_call | solution.py:608
where the time goes:
time: 137 us
  Pallas kernels  136 us (99%)
    pallas_call x1, Pallas kernels, body(): pl.pallas_call(kernel, out_shape=(jax.ShapeDtypeStruct((1, 1), F32), near...  133 us
    pallas_call x1, Pallas kernels, body(): pl.pallas_call(finish, out_shape=(jax.ShapeDtypeStruct((1, 1), F32), big,...  3.64 us

commit v1 on v0

--- a/solution.py
+++ b/solution.py
@@ -429,21 +429,29 @@
             a_next(0, 2)
             a_next(1, 1)
 
-        pair_in(t)
-
         @pl.when(t < 8)
         def _():
+            pair_in(t)
+
+        @pl.when(t < 8)
+        def _():
             a_step(t, 1)
 
         @pl.when(t == 7)
         def _():
             a_last(0)
 
+        @pl.when(t < 8)
+        def _():
+            pair(t, 0)
+
         @pl.when((t >= 1) & (t < 9))
         def _():
             b_next(t - 1, 1)
 
-        pair(t, 0)
+        @pl.when(t < 8)
+        def _():
+            pair(t, 1)
 
         @pl.when((t >= 2) & (t < 10))
         def _():
@@ -453,7 +461,6 @@
         def _():
             b_z(t - 3)
 
-        pair(t, 1)
         return carry
 
     lax.fori_loop(0, 10, tick, 0)
@@ -506,8 +513,14 @@
         lo = 2 * AW + way * BW
         fsum[:, :, lo : lo + BW] = (slot[...].astype(F32) + val).astype(BF16)
     to_y(1)
+    pair_in(8)
+    pair(8, 0)
     from_y(0)
+    pair(8, 1)
     from_y(1)
+    pair_in(9)
+    pair(9, 0)
+    pair(9, 1)
     from_x(0)
     from_x(1)
     from_sibling(0)

time: 137 us -> 136 us (level)
  no operation moved by 1% of the time
where the time goes in v1:
time: 136 us
  Pallas kernels  135 us (99%)
    pallas_call x1, Pallas kernels, body(): pl.pallas_call(kernel, out_shape=(jax.ShapeDtypeStruct((1, 1), F32), near...  131 us
    pallas_call x1, Pallas kernels, body(): pl.pallas_call(finish, out_shape=(jax.ShapeDtypeStruct((1, 1), F32), big,...  3.64 us

profile of v1, /device:TPU:1, one launch (start us, length us, event | category | flops | bytes accessed | tf_op | source)
XLA Modules:
  0.0 135.9 jit_solution(4826774817043853983)
XLA Ops:
  0.6 131.5 %step.1 = (f32[1,1]{1,0:T(1,128)}, bf16[256,2560]{1,0:T(8,128)(2,1)S(1)}, bf16[256,2560]{1,0:T(8,128)(2,1)S(1)}, bf16[256,2560]{1,0:T(8,128)(2,1)S(1)}, bf16[4,40,2560]{2,1,0:T(8,128)(2,1)S(1)}) custom-call(bf16[256,2560]{1,0:T(8,128)(2,1)} %bitcast.11, bf16[256,2560]{1,0:T(8,128)(2,1)} %bitcast.12, bf16[256,2560]{1,0:T(8,128)(2,1)} %bitcast.13, ...), custom_call_target="tpu_custom_call" | custom-call | tf_op jit(solution)/shard_map/step/pallas_call | solution.py:567
  132.1 3.6 %finish.1 = (f32[1,1]{1,0:T(1,128)}, bf16[256,2560]{1,0:T(8,128)(2,1)}, bf16[256,2560]{1,0:T(8,128)(2,1)}, bf16[256,2560]{1,0:T(8,128)(2,1)}, f32[160,2560]{1,0:T(8,128)}) custom-call(f32[1,1]{1,0:T(1,128)} %get-tuple-element.15.loss_in, bf16[256,2560]{1,0:T(8,128)(2,1)S(1)} %get-tuple-element.16.dq, bf16[256,2560]{1,0:T(8,128)(2,1)S(1)} %get-tuple-element.17.dk, ...), custom_call_target="tpu_custom_call" | custom-call | tf_op jit(solution)/shard_map/finish/pallas_call | solution.py:621
